TPU v7x, 256 devices: a whole 4x4x8 slice. The times are simulated.
256 devices in a mesh: seq: 32 (over z, y), tp: 8 (over x, core).
Axes of the slice: x: 4, y: 4, z: 8, core: 2. Of those that a mesh axis runs over, the one named last changes fastest.
Arguments:
- tokens: bfloat16 [16384, 4096], P('seq'), may hold values from -80 to 80
- norm_gain: float32 [4096], replicated, may hold values from 0.1 to 1.9
- query_weight: bfloat16 [4096, 4096], P(None, 'tp'), may hold values from -1 to 1
- key_weight: bfloat16 [4096, 1024], P(None, 'tp'), may hold values from -8 to 8
- value_weight: bfloat16 [4096, 1024], P(None, 'tp'), may hold values from -0.09375 to 0.09375
- out_weight: bfloat16 [4096, 4096], P(None, 'tp'), may hold values from -1 to 1
- segments: int32 [16384], replicated, may hold values from 0 to 2, never falling along the last dimension, each value on 1 to 8192 neighbouring positions
Outputs:
- attn_out: bfloat16 [16384, 4096], P('seq', 'tp')
All inputs are finite; a program needn't handle non-finite values.
Results may differ from a plain program's by a relative error of at most 0.013.
The roundings to bfloat16 on the way count: a program that leaves them out, or rounds other values in their place, can miss the bound.
Values may be sent and summed in bfloat16 or wider, within the bound.
A program may use at most 128 MiB of HBM per device.

v0:
```python
import math

import jax
import jax.numpy as jnp
from jax import lax
from jax.sharding import PartitionSpec as P

HEAD_DIM = 128
WINDOW = 4096


def shifted(value, axis, steps):
    count = lax.axis_size(axis)
    leading, last = (max(0, -steps), min(count, count - steps))
    return lax.ppermute(value, axis, [(source, source + steps) for source in range(leading, last)])


def rotate(vectors, positions):
    half_dim = vectors.shape[-1] // 2
    freqs = 10000.0 ** (-(jnp.arange(half_dim, dtype=jnp.float32) * 2.0 / vectors.shape[-1]))
    angles = positions[:, None] * freqs[None, :]
    cosine = jnp.cos(angles)[:, None, :]
    sine_part = jnp.sin(angles)[:, None, :]
    first = vectors[..., :half_dim]
    second = vectors[..., half_dim:]
    return jnp.concatenate(
        [first * cosine - second * sine_part, second * cosine + first * sine_part], axis=-1
    )


def project(normed, weight, positions):
    product = jnp.dot(normed, weight, preferred_element_type=jnp.float32)
    shaped = product.reshape(product.shape[0], -1, HEAD_DIM)
    return rotate(shaped, positions).astype(jnp.bfloat16)


def attend(queries, keys, values, allowed):
    block_rows, query_heads, head_size = queries.shape
    value_heads = keys.shape[1]
    grouped = queries.reshape(block_rows, value_heads, query_heads // value_heads, head_size)
    scores = jnp.einsum(
        "tkgd,skd->kgts", grouped, keys, preferred_element_type=jnp.float32
    ) / math.sqrt(head_size)
    scores = jnp.where(allowed[None, None], scores, jnp.float32(-1e30))
    peak = jnp.max(scores, axis=-1, keepdims=True)
    weights = jnp.exp(scores - peak)
    totals = jnp.sum(weights, axis=-1, keepdims=True)
    probabilities = (weights / totals).astype(jnp.bfloat16)
    attended = jnp.einsum(
        "kgts,skd->tkgd", probabilities, values, preferred_element_type=jnp.float32
    )
    return attended.reshape(block_rows, query_heads * head_size).astype(jnp.bfloat16)


def shards(tokens, norm_gain, query_weight, key_weight, value_weight, out_weight, segments):
    block_rows = tokens.shape[0]
    seq_index = lax.axis_index("seq")
    seq_count = lax.axis_size("seq")
    halo_blocks = min((WINDOW + block_rows - 2) // block_rows, seq_count - 1)
    widened = tokens.astype(jnp.float32)
    scale = lax.rsqrt(jnp.mean(widened * widened, axis=-1, keepdims=True) + 1e-05)
    normed = (widened * scale * norm_gain[None, :]).astype(jnp.bfloat16)
    first_token = seq_index * block_rows
    positions = (first_token + jnp.arange(block_rows, dtype=jnp.int32)).astype(jnp.float32)
    queries = project(normed, query_weight, positions)
    keys = project(normed, key_weight, positions)
    value_heads = keys.shape[1]
    values = jnp.dot(normed, value_weight, preferred_element_type=jnp.float32).astype(jnp.bfloat16)
    key_width = value_heads * HEAD_DIM
    key_value = jnp.concatenate([keys.reshape(block_rows, key_width), values], axis=1)
    front = halo_blocks * block_rows
    known_blocks = key_value
    gathered_count = 0
    while gathered_count < halo_blocks:
        taking = min(gathered_count + 1, halo_blocks - gathered_count)
        outgoing = known_blocks[known_blocks.shape[0] - taking * block_rows :]
        incoming = shifted(outgoing, "seq", gathered_count + 1)
        known_blocks = jnp.concatenate([incoming, known_blocks], axis=0)
        gathered_count = gathered_count + taking
    before = known_blocks[:front]
    window_rows = jnp.concatenate([before, key_value], axis=0)
    span = window_rows.shape[0]
    window_keys = window_rows[:, :key_width].reshape(span, value_heads, HEAD_DIM)
    window_values = window_rows[:, key_width:].reshape(span, value_heads, HEAD_DIM)
    padded_segments = jnp.concatenate([jnp.full((front,), -1, jnp.int32), segments], axis=0)
    start_index = seq_index * block_rows
    key_segments = lax.dynamic_slice_in_dim(padded_segments, start_index, span, 0)
    query_segments = lax.dynamic_slice_in_dim(segments, start_index, block_rows, 0)
    query_pos = start_index + jnp.arange(block_rows, dtype=jnp.int32)
    key_pos = start_index - front + jnp.arange(span, dtype=jnp.int32)
    distance = query_pos[:, None] - key_pos[None, :]
    allowed = (
        (distance >= 0) & (distance < WINDOW) & (key_segments[None, :] == query_segments[:, None])
    )
    attended = attend(queries, window_keys, window_values, allowed)
    projected = jnp.dot(
        lax.all_gather(attended, "tp", axis=1, tiled=True),
        out_weight,
        preferred_element_type=jnp.float32,
    )
    return projected.astype(jnp.bfloat16)


def solution(mesh):
    return jax.shard_map(
        shards,
        mesh=mesh,
        in_specs=(
            P("seq", None),
            P(),
            P(None, "tp"),
            P(None, "tp"),
            P(None, "tp"),
            P(None, "tp"),
            P(),
        ),
        out_specs=P("seq", "tp"),
        check_vma=False,
    )
```

profile of v0, /device:TPU:65, one launch (start us, length us, event | category | flops | bytes accessed | tf_op | source)
XLA Modules:
  0.0 179.1 jit_solution(8147630564713881535)
XLA Ops:
  6.6 3.2 %fusion.6 = f32[512]{0:T(512)S(1)} fusion(bf16[512,4096]{1,0:T(8,128)(2,1)} %param.7), kind=kLoop, calls=%fused_computation.13 | loop fusion | flops 6290944 | bytes 4196352 | tf_op jit(solution)/shard_map/reduce_sum | solution.py:61
  9.8 0.5 copy-done.2
  10.3 1.6 convolution_convert_fusion.1
  12.0 1.6 convolution_bitcast_fusion
  13.6 0.6 fusion.25
  14.2 0.7 pad_maximum_fusion
  14.9 3.2 %collective-permute-start.1 = (bf16[512,256]{0,1:T(8,128)(2,1)}, bf16[512,256]{0,1:T(8,128)(2,1)S(1)}, u32[]{:S(2)}, u32[]{:S(2)}) collective-permute-start(bf16[512,256]{0,1:T(8,128)(2,1)} %pad_maximum_fusion), channel_id=1, source_target_pairs={{0,8},{8,16},{16,24},{24,32},{32,40},{40,48},{48,56},{56,64},{64,7... | collective-permute-start | bytes 786440 | tf_op jit(solution)/shard_map/ppermute | solution.py:15
  18.1 6.1 %collective-permute-start = (bf16[512,256]{0,1:T(8,128)(2,1)}, bf16[512,256]{0,1:T(8,128)(2,1)}, u32[]{:S(2)}, u32[]{:S(2)}) collective-permute-start(bf16[512,256]{0,1:T(8,128)(2,1)} %pad_maximum_fusion), channel_id=1, source_target_pairs={{0,64},{8,72},{16,80},{24,88},{32,96},{40,104},{48,112},{56,120},{... | collective-permute-start | bytes 786440 | tf_op jit(solution)/shard_map/ppermute | solution.py:15
  24.3 0.1 dynamic_slice.7
  24.3 0.1 pad_dynamic-slice_fusion
  24.4 1.9 %collective-permute-done.1 = bf16[512,256]{0,1:T(8,128)(2,1)S(1)} collective-permute-done((bf16[512,256]{0,1:T(8,128)(2,1)}, bf16[512,256]{0,1:T(8,128)(2,1)S(1)}, u32[]{:S(2)}, u32[]{:S(2)}) %collective-permute-start.1) | collective-permute-done | bytes 262176 | tf_op jit(solution)/shard_map/ppermute | solution.py:15
  26.3 0.1 maximum_maximum_fusion.1
  26.4 3.0 %collective-permute-start.2 = (bf16[1024,256]{0,1:T(8,128)(2,1)S(1)}, bf16[1024,256]{0,1:T(8,128)(2,1)S(1)}, u32[]{:S(2)}, u32[]{:S(2)}) collective-permute-start(bf16[1024,256]{0,1:T(8,128)(2,1)S(1)} %maximum_maximum_fusion.1), channel_id=1, source_target_pairs={{0,16},{8,24},{16,32},{24,40},{32,48},{40,56},{48,64},{56,72},{64,... | collective-permute-start | bytes 1572872 | tf_op jit(solution)/shard_map/ppermute | solution.py:15
  29.3 3.8 %fusion.5 = pred[512,4608]{0,1:T(8,128)(4,1)S(1)} fusion(s32[512]{0:T(512)S(1)} %dynamic_slice.7, s32[4608]{0:T(1024)S(1)} %get-tuple-element.16, s32[512]{0:T(512)S(1)} %iota_add_fusion.1, s32[4608]{0:T(1024)S(1)} %get-tuple-element.15), kind=kLoop, calls=%fused_computation.12 | loop fusion | flops 14155776 | bytes 2400256 | tf_op jit(solution)/shard_map/and | solution.py:93
  33.1 11.7 %collective-permute-done.2 = bf16[1024,256]{0,1:T(8,128)(2,1)S(1)} collective-permute-done((bf16[1024,256]{0,1:T(8,128)(2,1)S(1)}, bf16[1024,256]{0,1:T(8,128)(2,1)S(1)}, u32[]{:S(2)}, u32[]{:S(2)}) %collective-permute-start.2) | collective-permute-done | bytes 524320 | tf_op jit(solution)/shard_map/ppermute | solution.py:15
  44.8 1.1 maximum_maximum_fusion
  45.9 7.6 %collective-permute-start.3 = (bf16[2048,256]{0,1:T(8,128)(2,1)}, bf16[2048,256]{0,1:T(8,128)(2,1)}, u32[]{:S(2)}, u32[]{:S(2)}) collective-permute-start(bf16[2048,256]{0,1:T(8,128)(2,1)} %maximum_maximum_fusion), channel_id=1, source_target_pairs={{0,32},{8,40},{16,48},{24,56},{32,64},{40,72},{48,80},{56,88},{64,... | collective-permute-start | bytes 3145736 | tf_op jit(solution)/shard_map/ppermute | solution.py:15
  53.6 4.8 %fusion.30 = f32[512,512]{0,1:T(8,128)S(1)} fusion(bf16[4096,512]{1,0:T(8,128)(2,1)} %param.9, bf16[512,4096]{1,0:T(8,128)(2,1)S(1)} %copy-done.3, f32[4096]{0:T(1024)S(1)} %copy-done.16, f32[512]{0:T(512)S(1)} %add_rsqrt_fusion), kind=kOutput, calls=%fused_computation.59 | convolution fusion | flops 2155872256 | bytes 9455616 | tf_op jit(solution)/shard_map/dot_general | solution.py:32
  58.4 1.1 fusion.34
  59.5 1.4 copy.16
  60.8 2.4 %copy.15 = f32[512,4,64]{2,0,1:T(8,128)} copy(f32[512,4,64]{0,2,1:T(8,128)} %get-tuple-element.8) | data formatting | bytes 1048576
  63.2 1.0 multiply_cosine_fusion
  64.2 1.5 subtract_convert_fusion
  65.7 1.0 constant_dynamic-update-slice_fusion.4
  66.7 7.9 %collective-permute-done.3 = bf16[2048,256]{0,1:T(8,128)(2,1)} collective-permute-done((bf16[2048,256]{0,1:T(8,128)(2,1)}, bf16[2048,256]{0,1:T(8,128)(2,1)}, u32[]{:S(2)}, u32[]{:S(2)}) %collective-permute-start.3) | collective-permute-done | bytes 1048608 | tf_op jit(solution)/shard_map/ppermute | solution.py:15
  74.6 1.3 constant_dynamic-update-slice_fusion.3
  76.1 15.3 %fusion.1 = (f32[4,512]{1,0:T(4,128)S(1)}, f32[4608,512,4]{1,0,2:T(8,128)}) fusion(pred[512,4608]{0,1:T(8,128)(4,1)S(1)} %fusion.5, bf16[512,4,64]{2,0,1:T(8,128)(2,1)S(1)} %get-tuple-element.6, bf16[512,4,64]{2,0,1:T(8,128)(2,1)S(1)} %get-tuple-element.5, bf16[4608,256]{0,1:T(8,128)(2,1)S(1)} %constant_dynamic-update-slice_fusion), kind=kOutput, calls=%fused_computation.4 | convolution fusion | flops 2445277184 | bytes 42344448 | tf_op jit(solution)/shard_map/tkgd,skd->kgts/dot_general | solution.py:41
  91.4 16.0 %fusion = f32[4,512]{1,0:T(4,128)S(1)} fusion(f32[4608,512,4]{1,0,2:T(8,128)} %get-tuple-element.14, f32[4,512]{1,0:T(4,128)S(1)} %get-tuple-element.13, pred[512,4608]{0,1:T(8,128)(4,1)S(1)} %fusion.5), kind=kLoop, calls=%fused_computation.3 | loop fusion | flops 37746688 | bytes 40124416 | tf_op jit(solution)/shard_map/reduce_sum | solution.py:47
  107.4 18.3 %fusion.9 = bf16[128,4,512]{2,0,1:T(8,128)(2,1)} fusion(f32[4,512]{1,0:T(4,128)S(1)} %fusion, f32[4,512]{1,0:T(4,128)S(1)} %get-tuple-element.13, f32[4608,512,4]{1,0,2:T(8,128)} %get-tuple-element.14, pred[512,4608]{0,1:T(8,128)(4,1)S(1)} %fusion.5, bf16[4608,256]{0,1:T(8,128)(2,1)} %copy-done.13), kind=kOutput, calls=%fused_computation.17 | convolution fusion | flops 2463367168 | bytes 41828352 | tf_op jit(solution)/shard_map/kgts,skd->tkgd/dot_general | solution.py:49
  125.7 0.0 all-gather.2.cloned.1.call-update
  125.8 39.9 %all-gather.2.cloned.1.call-done = bf16[512,4096]{0,1:T(8,128)(2,1)} async-done(((bf16[512,512]{0,1:T(8,128)(2,1)}), bf16[512,4096]{0,1:T(8,128)(2,1)}) %all-gather.2.cloned.1.call-update) | async-done | bytes 4194320 | tf_op jit(solution)/shard_map/all_gather | solution.py:97
  165.7 6.6 %convolution_convert_fusion = bf16[512,512]{1,0:T(8,128)(2,1)} fusion(bf16[512,4096]{0,1:T(8,128)(2,1)} %all-gather.2.cloned.1.call-done, bf16[4096,512]{1,0:T(8,128)(2,1)} %param.12), kind=kOutput, calls=%fused_computation.16 | convolution fusion | flops 2147745792 | bytes 8912896 | tf_op jit(solution)/shard_map/dot_general | solution.py:96
  (42 shorter events, 0.2 us)
Async XLA Ops:
  6.5 3.3 %copy-start = (bf16[4096,128]{1,0:T(8,128)(2,1)S(1)}, bf16[4096,128]{1,0:T(8,128)(2,1)}, u32[]{:S(2)}) copy-start(bf16[4096,128]{1,0:T(8,128)(2,1)} %param.11) | copy-start | bytes 3145732
  6.5 3.3 %copy-start.15 = (f32[4096]{0:T(1024)S(1)}, f32[4096]{0:T(1024)}, u32[]{:S(2)}) copy-start(f32[4096]{0:T(1024)} %param.8) | copy-start | bytes 49156
  6.5 159.1 %all-gather.2.cloned.1.call-start = ((), (), s32[]{:S(2)}) async-start(), calls=%async_computation | async-start | bytes 4718592 | tf_op jit(solution)/shard_map/all_gather | solution.py:97
  6.6 3.8 %copy-start.2 = (bf16[512,4096]{1,0:T(8,128)(2,1)S(1)}, bf16[512,4096]{1,0:T(8,128)(2,1)}, u32[]{:S(2)}) copy-start(bf16[512,4096]{1,0:T(8,128)(2,1)} %param.7) | copy-start | bytes 12582916
  10.3 1.6 copy-start.14
  12.0 12.3 %copy-start.12 = (s32[16384]{0:T(1024)S(1)}, s32[16384]{0:T(1024)}, u32[]{:S(2)}) copy-start(s32[16384]{0:T(1024)} %param.13) | copy-start | bytes 196612
  13.6 40.0 %copy-start.16 = (f32[4096]{0:T(1024)S(1)}, f32[4096]{0:T(1024)}, u32[]{:S(2)}) copy-start(f32[4096]{0:T(1024)} %param.8) | copy-start | bytes 49156
  14.2 44.2 %copy-start.8 = (bf16[512,64]{0,1:T(8,128)(2,1)}, bf16[512,64]{0,1:T(8,128)(2,1)S(1)}, u32[]{:S(2)}) copy-start(bf16[512,64]{0,1:T(8,128)(2,1)S(1)} %get-tuple-element.9) | copy-start | bytes 196612
  14.2 44.2 %copy-start.10 = (bf16[512,64]{0,1:T(8,128)(2,1)}, bf16[512,64]{0,1:T(8,128)(2,1)S(1)}, u32[]{:S(2)}) copy-start(bf16[512,64]{0,1:T(8,128)(2,1)S(1)} %get-tuple-element.10) | copy-start | bytes 196612
  14.9 11.4 %collective-permute-start.1 = (bf16[512,256]{0,1:T(8,128)(2,1)}, bf16[512,256]{0,1:T(8,128)(2,1)S(1)}, u32[]{:S(2)}, u32[]{:S(2)}) collective-permute-start(bf16[512,256]{0,1:T(8,128)(2,1)} %pad_maximum_fusion), channel_id=1, source_target_pairs={{0,8},{8,16},{16,24},{24,32},{32,40},{40,48},{48,56},{56,64},{64,7... | collective-permute-start | bytes 786440 | tf_op jit(solution)/shard_map/ppermute | solution.py:15
  18.1 47.6 %collective-permute-start = (bf16[512,256]{0,1:T(8,128)(2,1)}, bf16[512,256]{0,1:T(8,128)(2,1)}, u32[]{:S(2)}, u32[]{:S(2)}) collective-permute-start(bf16[512,256]{0,1:T(8,128)(2,1)} %pad_maximum_fusion), channel_id=1, source_target_pairs={{0,64},{8,72},{16,80},{24,88},{32,96},{40,104},{48,112},{56,120},{... | collective-permute-start | bytes 786440 | tf_op jit(solution)/shard_map/ppermute | solution.py:15
  24.2 29.3 %copy-start.3 = (bf16[512,4096]{1,0:T(8,128)(2,1)S(1)}, bf16[512,4096]{1,0:T(8,128)(2,1)}, u32[]{:S(2)}) copy-start(bf16[512,4096]{1,0:T(8,128)(2,1)} %param.7) | copy-start | bytes 12582916
  26.3 32.1 %copy-start.4 = (bf16[512,256]{0,1:T(8,128)(2,1)}, bf16[512,256]{0,1:T(8,128)(2,1)S(1)}, u32[]{:S(2)}) copy-start(bf16[512,256]{0,1:T(8,128)(2,1)S(1)} %collective-permute-done.1) | copy-start | bytes 786436
  26.4 18.4 %collective-permute-start.2 = (bf16[1024,256]{0,1:T(8,128)(2,1)S(1)}, bf16[1024,256]{0,1:T(8,128)(2,1)S(1)}, u32[]{:S(2)}, u32[]{:S(2)}) collective-permute-start(bf16[1024,256]{0,1:T(8,128)(2,1)S(1)} %maximum_maximum_fusion.1), channel_id=1, source_target_pairs={{0,16},{8,24},{16,32},{24,40},{32,48},{40,56},{48,64},{56,72},{64,... | collective-permute-start | bytes 1572872 | tf_op jit(solution)/shard_map/ppermute | solution.py:15
  44.8 13.6 %copy-start.6 = (bf16[1024,256]{0,1:T(8,128)(2,1)}, bf16[1024,256]{0,1:T(8,128)(2,1)S(1)}, u32[]{:S(2)}) copy-start(bf16[1024,256]{0,1:T(8,128)(2,1)S(1)} %collective-permute-done.2) | copy-start | bytes 1572868
  45.9 28.7 %collective-permute-start.3 = (bf16[2048,256]{0,1:T(8,128)(2,1)}, bf16[2048,256]{0,1:T(8,128)(2,1)}, u32[]{:S(2)}, u32[]{:S(2)}) collective-permute-start(bf16[2048,256]{0,1:T(8,128)(2,1)} %maximum_maximum_fusion), channel_id=1, source_target_pairs={{0,32},{8,40},{16,48},{24,56},{32,64},{40,72},{48,80},{56,88},{64,... | collective-permute-start | bytes 3145736 | tf_op jit(solution)/shard_map/ppermute | solution.py:15
  63.2 12.7 %copy-start.7 = (bf16[1024,256]{0,1:T(8,128)(2,1)S(1)}, bf16[1024,256]{0,1:T(8,128)(2,1)}, u32[]{:S(2)}) copy-start(bf16[1024,256]{0,1:T(8,128)(2,1)} %copy-done.6) | copy-start | bytes 1572868
  63.2 12.8 %copy-start.5 = (bf16[512,256]{0,1:T(8,128)(2,1)S(1)}, bf16[512,256]{0,1:T(8,128)(2,1)}, u32[]{:S(2)}) copy-start(bf16[512,256]{0,1:T(8,128)(2,1)} %copy-done.4) | copy-start | bytes 786436
  63.2 12.8 %copy-start.9 = (bf16[512,64]{0,1:T(8,128)(2,1)S(1)}, bf16[512,64]{0,1:T(8,128)(2,1)}, u32[]{:S(2)}) copy-start(bf16[512,64]{0,1:T(8,128)(2,1)} %copy-done.8) | copy-start | bytes 196612
  63.2 12.8 %copy-start.11 = (bf16[512,64]{0,1:T(8,128)(2,1)S(1)}, bf16[512,64]{0,1:T(8,128)(2,1)}, u32[]{:S(2)}) copy-start(bf16[512,64]{0,1:T(8,128)(2,1)} %copy-done.10) | copy-start | bytes 196612
  76.0 15.3 %copy-start.13 = (bf16[4608,256]{0,1:T(8,128)(2,1)}, bf16[4608,256]{0,1:T(8,128)(2,1)S(1)}, u32[]{:S(2)}) copy-start(bf16[4608,256]{0,1:T(8,128)(2,1)S(1)} %constant_dynamic-update-slice_fusion) | copy-start | bytes 7077892
  125.7 46.5 %copy-start.1 = (bf16[4096,128]{1,0:T(8,128)(2,1)S(1)}, bf16[4096,128]{1,0:T(8,128)(2,1)}, u32[]{:S(2)}) copy-start(bf16[4096,128]{1,0:T(8,128)(2,1)} %param.11) | copy-start | bytes 3145732
Sparse Core Ops, SparseCore 0:
  125.9 39.7 all-gather.1
where the time goes:
time: 181 us; the launch traced here: 179 us
  waiting for transfers between devices  61.4 us (34%)
  matrix products  48.2 us (27%)
  other arithmetic  28.1 us (16%)
  starting transfers between devices  19.9 us (11%)
  between operations  13.7 us (8%)
  local copies, waits for them, and re-layouts  7.75 us (4%)
    all_gather x1, waiting for transfers between devices, shards(): lax.all_gather(attended, 'tp', axis=1, tiled=True)  39.9 us
    ppermute x4, waiting for transfers between devices, shifted(): lax.ppermute(value, axis, [(source, source + steps) for source in range(l...  21.5 us
    ppermute x4, starting transfers between devices, shifted(): lax.ppermute(value, axis, [(source, source + steps) for source in range(l...  19.9 us
    dot_general x1, matrix products, attend(): jnp.einsum('kgts,skd->tkgd', probabilities, values, preferred_element_typ...  18.3 us
    reduce_sum x1, other arithmetic, attend(): totals = jnp.sum(weights, axis=-1, keepdims=True)  16 us
    dot_general x1, matrix products, attend(): jnp.einsum('tkgd,skd->kgts', grouped, keys, preferred_element_type=jnp.fl...  15.3 us
    unnamed x40, local copies, waits for them, and re-layouts  6.61 us
    dot_general x1, matrix products, shards(): jnp.dot(lax.all_gather(attended, 'tp', axis=1, tiled=True), out_weight, p...  6.61 us
  transfers between devices with their start and end apart: 5, of which 4 were waited for; matrix products, arithmetic and copies ran while one was open for 10% of the time, Pallas kernels for 0%

commit v1 on v0

v1 whole, which is shorter than its diff:
```python
import math

import jax
import jax.numpy as jnp
from jax import lax
from jax.experimental import pallas as pl
from jax.experimental.pallas import tpu as pltpu
from jax.sharding import PartitionSpec as P

HEAD_DIM = 128
WINDOW = 4096
TILES = 4
NB = 3
Z1, Z2, LA, L1, RA, R1, LX, RX = range(1, 9)
F32 = jnp.float32
BF16 = jnp.bfloat16


def pick(y, options):
    value = jnp.int32(options[3])
    for i in (2, 1, 0):
        value = jnp.where(y == i, jnp.int32(options[i]), value)
    return value


def kernel(tok_hbm, gain_ref, cos_ref, sin_ref, lo_ref, wq_hbm, wk_hbm, wv_hbm, wo_hbm, out_ref,
           xs, nrm, wq, wkv, wo, kv, qs, m_s, acc, gb,
           tok_sem, w_sem, ksend, krecv, gsend, grecv):
    rows, width = xs.shape
    heads = wq.shape[1] // HEAD_DIM
    tile = rows // TILES
    seq = lax.axis_index("seq")
    tp = lax.axis_index("tp")
    y = lax.rem(seq, 4)
    z = seq // 4
    row0 = z * 4
    z_next = lax.rem(seq + 4, 32)
    z_prev = lax.rem(seq + 28, 32)
    right = row0 + lax.rem(y + 1, 4)
    left = row0 + lax.rem(y + 3, 4)
    core = lax.rem(tp, 2)
    x_right = lax.rem(tp + 2, 8)
    x_left = lax.rem(tp + 6, 8)
    sib = tp + 1 - 2 * core
    opposite = lax.rem(tp + 4, 8)

    tok_copies = [
        pltpu.make_async_copy(tok_hbm.at[pl.ds(i * tile, tile)], xs.at[pl.ds(i * tile, tile)], tok_sem.at[i])
        for i in range(TILES)
    ]
    wk_copy = pltpu.make_async_copy(wk_hbm, wkv.at[:, pl.ds(0, HEAD_DIM)], w_sem.at[0])
    wv_copy = pltpu.make_async_copy(wv_hbm, wkv.at[:, pl.ds(HEAD_DIM, HEAD_DIM)], w_sem.at[1])
    wq_copy = pltpu.make_async_copy(wq_hbm, wq, w_sem.at[2])
    wo_copy = pltpu.make_async_copy(wo_hbm, wo, w_sem.at[3])
    for copy in tok_copies + [wk_copy, wv_copy, wq_copy, wo_copy]:
        copy.start()

    barrier = pltpu.get_barrier_semaphore()
    for where in ({"seq": z_next}, {"seq": z_prev}, {"seq": right}, {"seq": left},
                  {"tp": x_right}, {"tp": x_left}, {"tp": sib}):
        pl.semaphore_signal(barrier, inc=1, device_id=where, device_id_type=pl.DeviceIdType.MESH)

    def norm_rows(i, carry):
        at = pl.ds(pl.multiple_of(i * 16, 16), 16)
        x = xs[at, :].astype(F32)
        scale = lax.rsqrt(jnp.mean(x * x, axis=-1, keepdims=True) + 1e-05)
        nrm[at, :] = (x * scale * gain_ref[...]).astype(BF16)
        return carry

    for i in range(TILES):
        tok_copies[i].wait()
        lax.fori_loop(i * (tile // 16), (i + 1) * (tile // 16), norm_rows, 0)

    def rotate(x, cosine, sine):
        return x * cosine + pltpu.roll(x, HEAD_DIM // 2, 1) * sine

    wk_copy.wait()
    wv_copy.wait()
    half = rows // 2
    for i in range(2):
        at = pl.ds(i * half, half)
        both = jnp.dot(nrm[at, :], wkv[...], preferred_element_type=F32)
        kv[0, at, :HEAD_DIM] = rotate(both[:, :HEAD_DIM], cos_ref[at, :], sin_ref[at, :]).astype(BF16)
        kv[0, at, HEAD_DIM:] = both[:, HEAD_DIM:].astype(BF16)

    pl.semaphore_wait(barrier, 7)

    def halo(message, source, where):
        return pltpu.make_async_remote_copy(
            src_ref=kv.at[source], dst_ref=kv.at[message],
            send_sem=ksend.at[message], recv_sem=krecv.at[message],
            device_id={"seq": where}, device_id_type=pl.DeviceIdType.MESH)

    halo(Z1, 0, z_next).start()

    @pl.when(y < 3)
    def _():
        halo(LA, 0, right).start()

    @pl.when(y == 0)
    def _():
        halo(RA, 0, left).start()

    wq_copy.wait()
    for pair in range(heads // 2):
        both = jnp.dot(nrm[...], wq[:, pair * 256:(pair + 1) * 256], preferred_element_type=F32)
        for j in range(2):
            h = pair * 2 + j
            q = rotate(both[:, j * 128:(j + 1) * 128], cos_ref[...], sin_ref[...]).astype(BF16)
            for t in range(TILES):
                qs[t, h * tile:(h + 1) * tile, :] = q[t * tile:(t + 1) * tile, :]

    factor = math.log2(math.e) / math.sqrt(HEAD_DIM)
    lanes = lax.broadcasted_iota(jnp.int32, (tile, HEAD_DIM), 1)
    ones = jnp.ones((rows, HEAD_DIM), BF16)
    column = lambda steps: lax.rem(y + steps + 4, 4)
    back = [0, 1, 2, pick(y, (2, 0, 0, 0)), 1, pick(y, (2, 2, 2, 0)), 1,
            pick(y, (1, 1, 0, 0)), pick(y, (2, 2, 1, 1))]
    side = [0, 0, 0, -1, -1, 1, 1, -2, 2]
    starts = [((z - back[s]) * 4 + column(side[s])) * rows for s in range(9)]

    def start_of(slot):
        value = starts[8]
        for s in range(7, -1, -1):
            value = jnp.where(slot == s, starts[s], value)
        return value

    def unit(t, slot, first):
        k = kv[slot, :, :HEAD_DIM]
        v = jnp.concatenate([kv[slot, :, HEAD_DIM:], ones], axis=1)
        low = lo_ref[pl.ds(pl.multiple_of(t * tile, tile), tile), :] - start_of(slot)
        s = lax.dot_general(qs[t], k, (((1,), (1,)), ((), ())), preferred_element_type=F32)
        keep = []
        for c in range(rows // 128):
            ok = lanes + c * 128 >= low
            if first:
                mine = lax.broadcasted_iota(jnp.int32, (tile, HEAD_DIM), 0) + t * tile
                ok = ok & (lanes + c * 128 <= mine)
            keep.append(ok)
        chunks = []
        for c in range(rows // 128):
            part = s[:, c * 128:(c + 1) * 128]
            part = jnp.concatenate(
                [jnp.where(keep[c], part[h * tile:(h + 1) * tile], F32(-1e30)) for h in range(heads)], axis=0)
            chunks.append(part)
        top = chunks[0]
        for part in chunks[1:]:
            top = jnp.maximum(top, part)
        peak = jnp.max(top, axis=1, keepdims=True) * factor
        peak = jnp.broadcast_to(peak, (heads * tile, HEAD_DIM))
        if not first:
            old = m_s[t]
            peak = jnp.maximum(old, peak)
        p = jnp.concatenate([jnp.exp2(part * factor - peak).astype(BF16) for part in chunks], axis=1)
        new = jnp.dot(p, v, preferred_element_type=F32)
        m_s[t] = peak
        if first:
            acc[t] = new
        else:
            decay = jnp.exp2(old - peak)
            acc[t, :, :HEAD_DIM] = acc[t, :, :HEAD_DIM] * decay + new[:, :HEAD_DIM]
            acc[t, :, HEAD_DIM:] = acc[t, :, HEAD_DIM:] * decay + new[:, HEAD_DIM:]

    def sweep(slot, first=False):
        def body(t, carry):
            unit(t, slot, first)
            return carry
        lax.fori_loop(0, TILES, body, 0)

    order = [pick(y, options) for options in zip(
        (Z1, Z2, L1, R1, LA, RA, LX, RX),
        (Z1, LA, Z2, L1, R1, RA, LX, RX),
        (Z1, LA, Z2, L1, R1, RA, LX, RX),
        (Z1, LA, RA, Z2, L1, R1, LX, RX))]
    inner = (y == 1) | (y == 2)
    relay_right = jnp.where(inner, LA, L1)
    relay_left = jnp.where(inner, RA, R1)

    def arrive(step):
        slot = order[step]
        halo(slot, slot, right).wait_recv()
        if step == 0:
            halo(Z2, Z1, z_next).start()
            halo(L1, Z1, right).start()
            halo(R1, Z1, left).start()
            return slot

        @pl.when((slot == Z2) & (y > 0))
        def _():
            halo(RA, Z2, left).start()

        @pl.when((slot == Z2) & (y == 3))
        def _():
            halo(LA, Z2, right).start()

        @pl.when(slot == relay_right)
        def _():
            halo(LX, relay_right, right).start()

        @pl.when(slot == relay_left)
        def _():
            halo(RX, relay_left, left).start()

        return slot

    sweep(0, True)
    for step in range(8 - NB):
        sweep(arrive(step))
    last = [arrive(step) for step in range(8 - NB, 8)]

    half_tile = tile // 2
    upper, lower = pl.ds(0, half_tile), pl.ds(half_tile, half_tile)
    everything = pl.ds(0, tile)
    gather_plan = (
        (0, 1, everything, x_right), (0, 2, everything, x_left), (0, 4, everything, sib),
        (1, 3, upper, x_right), (2, 3, lower, x_left),
        (1, 5, everything, sib), (2, 6, everything, sib),
        (3, 7, upper, sib), (3, 7, lower, sib))

    def gather(t, message):
        source, target, part, where = gather_plan[message]
        return pltpu.make_async_remote_copy(
            src_ref=gb.at[t, source, part], dst_ref=gb.at[t, target, part],
            send_sem=gsend.at[t, message], recv_sem=grecv.at[t, message],
            device_id={"tp": where}, device_id_type=pl.DeviceIdType.MESH)

    def finish(t):
        result = (acc[t, :, :HEAD_DIM] / acc[t, :, HEAD_DIM:]).astype(BF16)
        for h in range(heads):
            gb[t, 0, :, h * 128:(h + 1) * 128] = result[h * tile:(h + 1) * tile]
        for message in (0, 1, 2):
            gather(t, message).start()

    def relay(t):
        gather(t, 0).wait_recv()
        gather(t, 3).start()
        gather(t, 5).start()
        gather(t, 1).wait_recv()
        gather(t, 4).start()
        gather(t, 6).start()

    def across(t):
        gather(t, 3).wait_recv()
        gather(t, 7).start()
        gather(t, 4).wait_recv()
        gather(t, 8).start()

    flip = lambda index: index + 1 - 2 * core
    owners = (tp, x_left, x_right, opposite, sib, flip(x_left), flip(x_right), flip(opposite))
    part_width = heads * HEAD_DIM

    def project(t):
        for message in (2, 5, 6, 7, 8):
            gather(t, message).wait_recv()
        total = jnp.zeros((tile, out_ref.shape[1]), F32)
        for i in range(8):
            at = pl.ds(pl.multiple_of(owners[i] * part_width, part_width), part_width)
            total += jnp.dot(gb[t, i], wo[at, :], preferred_element_type=F32)
        out_ref[pl.ds(pl.multiple_of(t * tile, tile), tile), :] = total.astype(BF16)

    wo_copy.wait()
    for t in range(TILES):
        for slot in last:
            unit(t, slot, False)
        finish(t)
        if t >= 1:
            relay(t - 1)
        if t >= 2:
            across(t - 2)
    project(0)
    relay(3)
    across(2)
    project(1)
    across(3)
    project(2)
    project(3)

    for t in range(TILES):
        for message in range(9):
            gather(t, message).wait_send()
    for message in range(1, 9):
        halo(message, message, right).wait_send()


def shards(tokens, norm_gain, query_weight, key_weight, value_weight, out_weight, segments):
    rows, width = tokens.shape
    heads = query_weight.shape[1] // HEAD_DIM
    first = lax.axis_index("seq") * rows
    indices = first + jnp.arange(rows, dtype=jnp.int32)
    half = HEAD_DIM // 2
    freqs = 10000.0 ** (-(jnp.arange(half, dtype=F32) * 2.0 / HEAD_DIM))
    angles = indices.astype(F32)[:, None] * freqs[None, :]
    cosine, sine = jnp.cos(angles), jnp.sin(angles)
    cosine = jnp.concatenate([cosine, cosine], axis=1)
    sine = jnp.concatenate([-sine, sine], axis=1)
    mine = lax.dynamic_slice_in_dim(segments, first, rows, 0)
    one = jnp.sum((segments < 1).astype(jnp.int32))
    two = jnp.sum((segments < 2).astype(jnp.int32))
    begin = jnp.where(mine == 0, 0, jnp.where(mine == 1, one, two))
    low = jnp.maximum(indices - (WINDOW - 1), begin)
    low = jnp.broadcast_to(low[:, None], (rows, HEAD_DIM))
    tile = rows // TILES
    vmem = pl.BlockSpec(memory_space=pltpu.VMEM)
    hbm = pl.BlockSpec(memory_space=pl.ANY)
    return pl.pallas_call(
        kernel,
        out_shape=jax.ShapeDtypeStruct((rows, out_weight.shape[1]), BF16),
        in_specs=[hbm, vmem, vmem, vmem, vmem, hbm, hbm, hbm, hbm],
        out_specs=vmem,
        scratch_shapes=[
            pltpu.VMEM((rows, width), BF16),
            pltpu.VMEM((rows, width), BF16),
            pltpu.VMEM(query_weight.shape, BF16),
            pltpu.VMEM((width, 2 * HEAD_DIM), BF16),
            pltpu.VMEM(out_weight.shape, BF16),
            pltpu.VMEM((9, rows, 2 * HEAD_DIM), BF16),
            pltpu.VMEM((TILES, heads * tile, HEAD_DIM), BF16),
            pltpu.VMEM((TILES, heads * tile, HEAD_DIM), F32),
            pltpu.VMEM((TILES, heads * tile, 2 * HEAD_DIM), F32),
            pltpu.VMEM((TILES, 8, tile, heads * HEAD_DIM), BF16),
            pltpu.SemaphoreType.DMA((TILES,)),
            pltpu.SemaphoreType.DMA((4,)),
            pltpu.SemaphoreType.DMA((9,)),
            pltpu.SemaphoreType.DMA((9,)),
            pltpu.SemaphoreType.DMA((TILES, 9)),
            pltpu.SemaphoreType.DMA((TILES, 9)),
        ],
        compiler_params=pltpu.CompilerParams(
            collective_id=0, has_side_effects=True, vmem_limit_bytes=56 << 20),
    )(tokens, norm_gain[None, :], cosine, sine, low, query_weight, key_weight, value_weight, out_weight)


def solution(mesh):
    return jax.shard_map(
        shards,
        mesh=mesh,
        in_specs=(
            P("seq", None),
            P(),
            P(None, "tp"),
            P(None, "tp"),
            P(None, "tp"),
            P(None, "tp"),
            P(),
        ),
        out_specs=P("seq", "tp"),
        check_vma=False,
    )
```

time: 181 us -> 81.2 us (0.45)
  the two profiles are of different devices: /device:TPU:65 before, /device:TPU:1 now
where the time goes in v1:
time: 81.2 us; the launch traced here: 80.9 us
  Pallas kernels  71.8 us (88%)
  other arithmetic  6.36 us (8%)
  local copies, waits for them, and re-layouts  2.72 us (3%)
    pallas_call x1, Pallas kernels, shards(): pl.pallas_call(kernel, out_shape=jax.ShapeDtypeStruct((rows, out_weight.s...  71.8 us
    max x1, other arithmetic, shards(): low = jnp.maximum(indices - (WINDOW - 1), begin)  2.1 us
    unnamed x1, local copies, waits for them, and re-layouts  1.87 us

profile of v1, /device:TPU:1, one launch (start us, length us, event | category | flops | bytes accessed | tf_op | source)
XLA Modules:
  0.0 80.9 jit_solution(15620996843395182962)
XLA Ops:
  0.0 1.6 %convert_reduce_fusion.1 = (s32[]{:T(128)}, s32[]{:T(128)}) fusion(s32[16384]{0:T(1024)} %param.13), kind=kLoop, calls=%fused_computation.6 | loop fusion | flops 98302 | bytes 65544 | tf_op jit(solution)/shard_map/reduce_sum | solution.py:297
  1.6 2.1 %select_maximum_fusion = (s32[512]{0:T(512)S(1)}, f32[512]{0:T(512)S(1)}) fusion(s32[16384]{0:T(1024)} %param.13, s32[]{:T(128)S(6)} %select_n.11, s32[]{:T(128)} %get-tuple-element.6, s32[]{:T(128)} %get-tuple-element.5, s32[]{:T(128)S(6)} %mul.9), kind=kLoop, calls=%fused_computation.7 | loop fusion | flops 4096 | bytes 6160 | tf_op jit(solution)/shard_map/max | solution.py:300
  3.7 0.8 %broadcast_in_dim.24.lo_ref = s32[512,128]{1,0:T(8,128)} broadcast(s32[512]{0:T(512)S(1)} %get-tuple-element.10), dimensions={0} | broadcast | bytes 264192 | tf_op jit(solution)/shard_map/broadcast_in_dim | solution.py:301
  4.5 1.0 %fusion = (f32[512,64]{1,0:T(8,128)S(1)}, f32[512,64]{1,0:T(8,128)S(1)}, f32[512,64]{1,0:T(8,128)S(1)}) fusion(f32[64]{0:T(128)S(1)} %negate_power_fusion, f32[512]{0:T(512)S(1)} %get-tuple-element.11), kind=kLoop, calls=%fused_computation.4 | loop fusion | flops 65536 | bytes 395520 | tf_op jit(solution)/shard_map/neg | solution.py:295
  5.5 0.8 %pad_maximum_fusion.1.sin_ref = f32[512,128]{1,0:T(8,128)} fusion(f32[512,64]{1,0:T(8,128)S(1)} %get-tuple-element.8, f32[512,64]{1,0:T(8,128)S(1)} %get-tuple-element.7), kind=kLoop, calls=%fused_computation.3 | loop fusion | flops 65536 | bytes 524288 | tf_op jit(solution)/shard_map/concatenate | solution.py:295
  6.4 0.8 %pad_maximum_fusion.cos_ref = f32[512,128]{1,0:T(8,128)} fusion(f32[512,64]{1,0:T(8,128)S(1)} %get-tuple-element.9), kind=kLoop, calls=%fused_computation.2 | loop fusion | flops 65536 | bytes 393216 | tf_op jit(solution)/shard_map/concatenate | solution.py:294
  7.2 71.8 %shard_map.73 = bf16[512,512]{1,0:T(8,128)(2,1)} custom-call(bf16[512,4096]{1,0:T(8,128)(2,1)} %tok_hbm.1, f32[1,4096]{1,0:T(1,128)} %bitcast.1, f32[512,128]{1,0:T(8,128)} %pad_maximum_fusion.cos_ref, f32[512,128]{1,0:T(8,128)} %pad_maximum_fusion.1.sin_ref, s32[512,128]{1,0:T(8,128)} %broadcast_in_dim.24.lo_ref, bf16[4096,512]{1,0:T(8,128)(2,1)} %wq_hbm.1, ...), custom_call_target="tpu_custom_call" | custom-call | tf_op jit(solution)/shard_map/pallas_call | solution.py:305
  79.1 1.9 %copy.9 = bf16[512,512]{1,0:T(8,128)(2,1)} copy(bf16[512,512]{1,0:T(8,128)(2,1)} %shard_map.73) | data formatting | bytes 1048576
  (1 shorter events, 0.0 us)

commit v2 on v1

v2 whole, which is shorter than its diff:
```python
import math

import jax
import jax.numpy as jnp
from jax import lax
from jax.experimental import pallas as pl
from jax.experimental.pallas import tpu as pltpu
from jax.sharding import PartitionSpec as P

HEAD_DIM = 128
WINDOW = 4096
TILES = 4
NB = 2
Z1, Z2, LA, L1, RA, R1, LX, RX = range(1, 9)
F32 = jnp.float32
BF16 = jnp.bfloat16


def pick(y, options):
    value = jnp.int32(options[3])
    for i in (2, 1, 0):
        value = jnp.where(y == i, jnp.int32(options[i]), value)
    return value


def kernel(tok_hbm, gain_ref, freq_ref, seg_ref, wq_hbm, wk_hbm, wv_hbm, wo_hbm, out_ref,
           xs, nrm, wq, wkv, wo, kv, qs, m_s, acc, gb, cos_s, sin_s, low_s,
           tok_sem, w_sem, ksend, krecv, gsend, grecv):
    rows, width = xs.shape
    heads = wq.shape[1] // HEAD_DIM
    tile = rows // TILES
    half = rows // 2
    seq = lax.axis_index("seq")
    tp = lax.axis_index("tp")
    y = lax.rem(seq, 4)
    z = seq // 4
    z_last = lax.axis_size("seq") // 4 - 1
    row0 = z * 4
    z_next = lax.rem(seq + 4, 32)
    z_prev = lax.rem(seq + 28, 32)
    right = row0 + lax.rem(y + 1, 4)
    left = row0 + lax.rem(y + 3, 4)
    core = lax.rem(tp, 2)
    x_right = lax.rem(tp + 2, 8)
    x_left = lax.rem(tp + 6, 8)
    sib = tp + 1 - 2 * core
    opposite = lax.rem(tp + 4, 8)

    tok_copies = [
        pltpu.make_async_copy(tok_hbm.at[pl.ds(i * tile, tile)], xs.at[pl.ds(i * tile, tile)], tok_sem.at[i])
        for i in range(TILES)
    ]
    wk_copy = pltpu.make_async_copy(wk_hbm, wkv.at[:, pl.ds(0, HEAD_DIM)], w_sem.at[0])
    wv_copy = pltpu.make_async_copy(wv_hbm, wkv.at[:, pl.ds(HEAD_DIM, HEAD_DIM)], w_sem.at[1])
    wq_copy = pltpu.make_async_copy(wq_hbm, wq, w_sem.at[2])
    wo_copy = pltpu.make_async_copy(wo_hbm, wo, w_sem.at[3])
    for copy in tok_copies[:2] + [wk_copy, wv_copy] + tok_copies[2:] + [wq_copy, wo_copy]:
        copy.start()

    barrier = pltpu.get_barrier_semaphore()
    for where in ({"seq": z_next}, {"seq": z_prev}, {"seq": right}, {"seq": left},
                  {"tp": x_right}, {"tp": x_left}, {"tp": sib}):
        pl.semaphore_signal(barrier, inc=1, device_id=where, device_id_type=pl.DeviceIdType.MESH)

    def count_below(value):
        hits = (seg_ref[...] < value).astype(F32)
        return jnp.sum(jnp.sum(hits, axis=0, keepdims=True), axis=1, keepdims=True).astype(jnp.int32)

    second, third = count_below(1), count_below(2)

    def tables(i, carry):
        at = pl.ds(pl.multiple_of(i * 64, 64), 64)
        position = seq * rows + i * 64 + lax.broadcasted_iota(jnp.int32, (64, HEAD_DIM), 0)
        angle = position.astype(F32) * freq_ref[...]
        lane = lax.broadcasted_iota(jnp.int32, (64, HEAD_DIM), 1)
        sine = jnp.sin(angle)
        cos_s[at, :] = jnp.cos(angle)
        sin_s[at, :] = jnp.where(lane < HEAD_DIM // 2, -sine, sine)
        begin = jnp.where(position < second, 0, jnp.where(position < third, second, third))
        low_s[at, :] = jnp.maximum(position - (WINDOW - 1), begin)
        return carry

    lax.fori_loop(0, rows // 64, tables, 0)

    back = [0, 1, 2, pick(y, (2, 0, 0, 0)), 1, pick(y, (2, 2, 2, 0)), 1,
            pick(y, (1, 1, 0, 0)), pick(y, (2, 2, 1, 1))]
    side = [0, 0, 0, -1, -1, 1, 1, -2, 2]
    starts = [((z - back[s]) * 4 + lax.rem(y + side[s] + 4, 4)) * rows for s in range(9)]
    for s in range(1, 9):
        @pl.when(z < back[s])
        def _():
            kv[s] = jnp.zeros(kv.shape[1:], BF16)

    def norm_rows(i, carry):
        at = pl.ds(pl.multiple_of(i * 16, 16), 16)
        x = xs[at, :].astype(F32)
        scale = lax.rsqrt(jnp.mean(x * x, axis=-1, keepdims=True) + 1e-05)
        nrm[at, :] = (x * scale * gain_ref[...]).astype(BF16)
        return carry

    def rotate(x, cosine, sine):
        return x * cosine + pltpu.roll(x, HEAD_DIM // 2, 1) * sine

    def halo(message, source, where, c):
        part = pl.ds(c * half, half)
        return pltpu.make_async_remote_copy(
            src_ref=kv.at[source, part], dst_ref=kv.at[message, part],
            send_sem=ksend.at[message, c], recv_sem=krecv.at[message, c],
            device_id={"seq": where}, device_id_type=pl.DeviceIdType.MESH)

    def send(condition, message, source, where, c):
        @pl.when(condition)
        def _():
            halo(message, source, where, c).start()

    def got(message, c, condition=None):
        valid = z >= back[message]
        @pl.when(valid if condition is None else valid & condition)
        def _():
            halo(message, message, right, c).wait_recv()

    for c in range(2):
        for i in range(c * TILES // 2, (c + 1) * TILES // 2):
            tok_copies[i].wait()
            lax.fori_loop(i * (tile // 16), (i + 1) * (tile // 16), norm_rows, 0, unroll=2)
        if c == 0:
            wk_copy.wait()
            wv_copy.wait()
        at = pl.ds(c * half, half)
        both = jnp.dot(nrm[at, :], wkv[...], preferred_element_type=F32)
        kv[0, at, :HEAD_DIM] = rotate(both[:, :HEAD_DIM], cos_s[at, :], sin_s[at, :]).astype(BF16)
        kv[0, at, HEAD_DIM:] = both[:, HEAD_DIM:].astype(BF16)
        if c == 0:
            pl.semaphore_wait(barrier, 7)
        send(z < z_last, Z1, 0, z_next, c)
        send(y < 3, LA, 0, right, c)
        send(y == 0, RA, 0, left, c)

    wq_copy.wait()
    for pair in range(heads // 2):
        both = jnp.dot(nrm[...], wq[:, pair * 256:(pair + 1) * 256], preferred_element_type=F32)
        for j in range(2):
            h = pair * 2 + j
            q = rotate(both[:, j * 128:(j + 1) * 128], cos_s[...], sin_s[...]).astype(BF16)
            for t in range(TILES):
                qs[t, h * tile:(h + 1) * tile, :] = q[t * tile:(t + 1) * tile, :]

    factor = math.log2(math.e) / math.sqrt(HEAD_DIM)
    lanes = lax.broadcasted_iota(jnp.int32, (tile, HEAD_DIM), 1)
    ones = jnp.ones((rows, HEAD_DIM), BF16)

    def start_of(slot):
        if isinstance(slot, int):
            return starts[slot]
        value = starts[8]
        for s in range(7, 0, -1):
            value = jnp.where(slot == s, starts[s], value)
        return value

    def unit(t, slot, first):
        k = kv[slot, :, :HEAD_DIM]
        v = jnp.concatenate([kv[slot, :, HEAD_DIM:], ones], axis=1)
        low = low_s[t * tile:(t + 1) * tile, :] - start_of(slot)
        s = lax.dot_general(qs[t], k, (((1,), (1,)), ((), ())), preferred_element_type=F32)
        chunks = []
        for c in range(rows // 128):
            ok = lanes + c * 128 >= low
            if first:
                mine = lax.broadcasted_iota(jnp.int32, (tile, HEAD_DIM), 0) + t * tile
                ok = ok & (lanes + c * 128 <= mine)
            part = s[:, c * 128:(c + 1) * 128]
            chunks.append(jnp.concatenate(
                [jnp.where(ok, part[h * tile:(h + 1) * tile], F32(-1e30)) for h in range(heads)], axis=0))
        top = chunks[0]
        for part in chunks[1:]:
            top = jnp.maximum(top, part)
        peak = jnp.max(top, axis=1, keepdims=True) * factor
        peak = jnp.broadcast_to(peak, (heads * tile, HEAD_DIM))
        if not first:
            old = m_s[t]
            peak = jnp.maximum(old, peak)
        p = jnp.concatenate([jnp.exp2(part * factor - peak).astype(BF16) for part in chunks], axis=1)
        new = jnp.dot(p, v, preferred_element_type=F32)
        m_s[t] = peak
        if first:
            acc[t] = new
        else:
            decay = jnp.exp2(old - peak)
            acc[t, :, :HEAD_DIM] = acc[t, :, :HEAD_DIM] * decay + new[:, :HEAD_DIM]
            acc[t, :, HEAD_DIM:] = acc[t, :, HEAD_DIM:] * decay + new[:, HEAD_DIM:]

    def sweep(slot, first=False):
        for t in range(TILES):
            unit(t, slot, first)

    order = [pick(y, options) for options in zip(
        (Z1, R1, Z2, L1, RA, LA), (Z1, LA, R1, Z2, L1, RA),
        (Z1, LA, R1, Z2, L1, RA), (Z1, LA, RA, R1, Z2, L1))]
    inner = (y == 1) | (y == 2)
    outer = (y == 0) | (y == 3)

    def from_z1(c):
        got(Z1, c)
        send((z >= 1) & (z < z_last), Z2, Z1, z_next, c)
        send(z >= 1, L1, Z1, right, c)
        send(z >= 1, R1, Z1, left, c)

    def from_z2(c):
        got(Z2, c)
        send((z >= 2) & (y > 0), RA, Z2, left, c)
        send((z >= 2) & (y == 3), LA, Z2, right, c)

    def from_la(c):
        got(LA, c, inner)
        send(inner, LX, LA, right, c)

    def from_r1(c, condition):
        got(R1, c, condition)
        send(condition & outer & (z >= 1), RX, R1, left, c)

    def from_l1(c):
        got(L1, c)
        send(outer & (z >= 1), LX, L1, right, c)

    def from_ra(c, condition):
        got(RA, c, condition)
        send(condition & inner & (z >= 2), RX, RA, left, c)

    from_z1(0)
    sweep(0, True)
    from_z1(1)
    from_la(0)
    from_la(1)
    sweep(order[0])
    from_z2(0)
    from_r1(0, y >= 0)
    from_r1(1, y == 0)
    got(LA, 0, y == 3)
    got(LA, 1, y == 3)
    sweep(order[1])
    from_z2(1)
    from_r1(1, y > 0)
    from_l1(0)
    from_ra(0, y == 3)
    from_ra(1, y == 3)
    sweep(order[2])
    from_l1(1)
    sweep(order[3])
    from_ra(0, y < 3)
    from_ra(1, y == 0)
    sweep(order[4])
    from_ra(1, inner)
    got(LA, 0, y == 0)
    got(LA, 1, y == 0)
    sweep(order[5])
    last = (LX, RX)
    for slot in last:
        got(slot, 0)
        got(slot, 1)

    half_tile = tile // 2
    upper, lower = pl.ds(0, half_tile), pl.ds(half_tile, half_tile)
    everything = pl.ds(0, tile)
    gather_plan = (
        (0, 1, everything, x_right), (0, 2, everything, x_left), (0, 4, everything, sib),
        (1, 3, upper, x_right), (2, 3, lower, x_left),
        (1, 5, everything, sib), (2, 6, everything, sib),
        (3, 7, upper, sib), (3, 7, lower, sib))

    def gather(t, message):
        source, target, part, where = gather_plan[message]
        return pltpu.make_async_remote_copy(
            src_ref=gb.at[t, source, part], dst_ref=gb.at[t, target, part],
            send_sem=gsend.at[t, message], recv_sem=grecv.at[t, message],
            device_id={"tp": where}, device_id_type=pl.DeviceIdType.MESH)

    def finish(t):
        result = (acc[t, :, :HEAD_DIM] / acc[t, :, HEAD_DIM:]).astype(BF16)
        for h in range(heads):
            gb[t, 0, :, h * 128:(h + 1) * 128] = result[h * tile:(h + 1) * tile]
        for message in (0, 1, 2):
            gather(t, message).start()

    def relay(t):
        gather(t, 0).wait_recv()
        gather(t, 3).start()
        gather(t, 5).start()
        gather(t, 1).wait_recv()
        gather(t, 4).start()
        gather(t, 6).start()

    def across(t):
        gather(t, 3).wait_recv()
        gather(t, 7).start()
        gather(t, 4).wait_recv()
        gather(t, 8).start()

    flip = lambda index: index + 1 - 2 * core
    owners = (tp, x_left, x_right, opposite, sib, flip(x_left), flip(x_right), flip(opposite))
    part_width = heads * HEAD_DIM

    def partial(t, sources):
        total = None
        for i in sources:
            at = pl.ds(pl.multiple_of(owners[i] * part_width, part_width), part_width)
            term = jnp.dot(gb[t, i], wo[at, :], preferred_element_type=F32)
            total = term if total is None else total + term
        return total

    def project(t, early=None):
        for message in (7, 8):
            gather(t, message).wait_recv()
        total = partial(t, (3, 7)) + (partial_of(t) if early is None else early)
        out_ref[t * tile:(t + 1) * tile, :] = total.astype(BF16)

    def partial_of(t):
        for message in (2, 5, 6):
            gather(t, message).wait_recv()
        return partial(t, (0, 1, 2, 4, 5, 6))

    wo_copy.wait()
    for t in range(TILES):
        for slot in last:
            unit(t, slot, False)
        finish(t)
        if t >= 2:
            relay(t - 2)
    relay(2)
    across(0)
    project(0)
    relay(3)
    across(1)
    project(1)
    across(2)
    project(2)
    early = partial_of(3)
    across(3)
    project(3, early)

    for t in range(TILES):
        for message in range(9):
            gather(t, message).wait_send()
    sent = {Z1: z < z_last, Z2: (z >= 1) & (z < z_last), LA: (y < 3) | (z >= 2), L1: z >= 1,
            LX: inner | (z >= 1), RA: (y == 0) | (z >= 2), R1: z >= 1,
            RX: (outer & (z >= 1)) | (inner & (z >= 2))}
    for message, condition in sent.items():
        @pl.when(condition)
        def _():
            for c in range(2):
                halo(message, message, right, c).wait_send()


def shards(tokens, norm_gain, query_weight, key_weight, value_weight, out_weight, segments):
    rows, width = tokens.shape
    heads = query_weight.shape[1] // HEAD_DIM
    freqs = 10000.0 ** (-(jnp.arange(HEAD_DIM // 2, dtype=F32) * 2.0 / HEAD_DIM))
    freqs = jnp.concatenate([freqs, freqs])[None, :]
    tile = rows // TILES
    vmem = pl.BlockSpec(memory_space=pltpu.VMEM)
    hbm = pl.BlockSpec(memory_space=pl.ANY)
    return pl.pallas_call(
        kernel,
        out_shape=jax.ShapeDtypeStruct((rows, out_weight.shape[1]), BF16),
        in_specs=[hbm, vmem, vmem, vmem, hbm, hbm, hbm, hbm],
        out_specs=vmem,
        scratch_shapes=[
            pltpu.VMEM((rows, width), BF16),
            pltpu.VMEM((rows, width), BF16),
            pltpu.VMEM(query_weight.shape, BF16),
            pltpu.VMEM((width, 2 * HEAD_DIM), BF16),
            pltpu.VMEM(out_weight.shape, BF16),
            pltpu.VMEM((9, rows, 2 * HEAD_DIM), BF16),
            pltpu.VMEM((TILES, heads * tile, HEAD_DIM), BF16),
            pltpu.VMEM((TILES, heads * tile, HEAD_DIM), F32),
            pltpu.VMEM((TILES, heads * tile, 2 * HEAD_DIM), F32),
            pltpu.VMEM((TILES, 8, tile, heads * HEAD_DIM), BF16),
            pltpu.VMEM((rows, HEAD_DIM), F32),
            pltpu.VMEM((rows, HEAD_DIM), F32),
            pltpu.VMEM((rows, HEAD_DIM), jnp.int32),
            pltpu.SemaphoreType.DMA((TILES,)),
            pltpu.SemaphoreType.DMA((4,)),
            pltpu.SemaphoreType.DMA((9, 2)),
            pltpu.SemaphoreType.DMA((9, 2)),
            pltpu.SemaphoreType.DMA((TILES, 9)),
            pltpu.SemaphoreType.DMA((TILES, 9)),
        ],
        compiler_params=pltpu.CompilerParams(
            collective_id=0, has_side_effects=True, vmem_limit_bytes=56 << 20),
    )(tokens, norm_gain[None, :], freqs, segments.reshape(-1, HEAD_DIM),
      query_weight, key_weight, value_weight, out_weight)


def solution(mesh):
    return jax.shard_map(
        shards,
        mesh=mesh,
        in_specs=(
            P("seq", None),
            P(),
            P(None, "tp"),
            P(None, "tp"),
            P(None, "tp"),
            P(None, "tp"),
            P(),
        ),
        out_specs=P("seq", "tp"),
        check_vma=False,
    )
```

time: 81.2 us -> 61.5 us (0.76)
  the two profiles are of different devices: /device:TPU:1 before, /device:TPU:65 now
where the time goes in v2:
time: 61.5 us; the launch traced here: 61.3 us
  Pallas kernels  58.9 us (96%)
  local copies, waits for them, and re-layouts  1.87 us (3%)
    pallas_call x1, Pallas kernels, shards(): pl.pallas_call(kernel, out_shape=jax.ShapeDtypeStruct((rows, out_weight.s...  58.9 us
    unnamed x1, local copies, waits for them, and re-layouts  1.87 us

profile of v2, /device:TPU:65, one launch (start us, length us, event | category | flops | bytes accessed | tf_op | source)
XLA Modules:
  0.0 61.3 jit_solution(11399955720128980970)
XLA Ops:
  0.0 0.6 maximum_bitcast_fusion.freq_ref
  0.6 58.9 %shard_map.73 = bf16[512,512]{1,0:T(8,128)(2,1)} custom-call(bf16[512,4096]{1,0:T(8,128)(2,1)} %tok_hbm.1, f32[1,4096]{1,0:T(1,128)} %bitcast.5, f32[1,128]{1,0:T(1,128)} %maximum_bitcast_fusion.freq_ref, s32[128,128]{1,0:T(8,128)} %bitcast.4, bf16[4096,512]{1,0:T(8,128)(2,1)} %wq_hbm.1, bf16[4096,128]{1,0:T(8,128)(2,1)} %wk_hbm.1, ...), custom_call_target="tpu_custom_call" | custom-call | tf_op jit(solution)/shard_map/pallas_call | solution.py:361
  59.5 1.9 %copy.9 = bf16[512,512]{1,0:T(8,128)(2,1)} copy(bf16[512,512]{1,0:T(8,128)(2,1)} %shard_map.73) | data formatting | bytes 1048576
  (1 shorter events, 0.0 us)

commit v3 on v2

--- a/solution.py
+++ b/solution.py
@@ -10,7 +10,6 @@
 HEAD_DIM = 128
 WINDOW = 4096
 TILES = 4
-NB = 2
 Z1, Z2, LA, L1, RA, R1, LX, RX = range(1, 9)
 F32 = jnp.float32
 BF16 = jnp.bfloat16
@@ -24,12 +23,11 @@
 
 
 def kernel(tok_hbm, gain_ref, freq_ref, seg_ref, wq_hbm, wk_hbm, wv_hbm, wo_hbm, out_ref,
-           xs, nrm, wq, wkv, wo, kv, qs, m_s, acc, gb, cos_s, sin_s, low_s,
+           xs, nrm, wq, wkv, wo, kv, qs, m_s, acc, gb, part, cos_s, sin_s, low_s,
            tok_sem, w_sem, ksend, krecv, gsend, grecv):
     rows, width = xs.shape
     heads = wq.shape[1] // HEAD_DIM
     tile = rows // TILES
-    half = rows // 2
     seq = lax.axis_index("seq")
     tp = lax.axis_index("tp")
     y = lax.rem(seq, 4)
@@ -68,19 +66,24 @@
 
     second, third = count_below(1), count_below(2)
 
-    def tables(i, carry):
-        at = pl.ds(pl.multiple_of(i * 64, 64), 64)
-        position = seq * rows + i * 64 + lax.broadcasted_iota(jnp.int32, (64, HEAD_DIM), 0)
-        angle = position.astype(F32) * freq_ref[...]
-        lane = lax.broadcasted_iota(jnp.int32, (64, HEAD_DIM), 1)
-        sine = jnp.sin(angle)
-        cos_s[at, :] = jnp.cos(angle)
-        sin_s[at, :] = jnp.where(lane < HEAD_DIM // 2, -sine, sine)
-        begin = jnp.where(position < second, 0, jnp.where(position < third, second, third))
-        low_s[at, :] = jnp.maximum(position - (WINDOW - 1), begin)
-        return carry
-
-    lax.fori_loop(0, rows // 64, tables, 0)
+    def tables(c):
+        small = tile // 2
+        shape = (small, HEAD_DIM)
+        lane = lax.broadcasted_iota(jnp.int32, shape, 1)
+        row = lax.broadcasted_iota(jnp.int32, shape, 0) + (seq * rows + c * tile)
+        front = lane < HEAD_DIM // 2
+        angle = jnp.where(front, row, row + small).astype(F32) * freq_ref[...]
+        cosine, sine = jnp.cos(angle), jnp.sin(angle)
+        other_cosine, other_sine = (pltpu.roll(value, HEAD_DIM // 2, 1) for value in (cosine, sine))
+        for i in range(2):
+            at = pl.ds(c * tile + i * small, small)
+            mine = front if i == 0 else ~front
+            turned = jnp.where(mine, sine, other_sine)
+            cos_s[at, :] = jnp.where(mine, cosine, other_cosine)
+            sin_s[at, :] = jnp.where(front, -turned, turned)
+            position = row + i * small
+            begin = jnp.where(position < second, 0, jnp.where(position < third, second, third))
+            low_s[at, :] = jnp.maximum(position - (WINDOW - 1), begin)
 
     back = [0, 1, 2, pick(y, (2, 0, 0, 0)), 1, pick(y, (2, 2, 2, 0)), 1,
             pick(y, (1, 1, 0, 0)), pick(y, (2, 2, 1, 1))]
@@ -101,32 +104,73 @@
     def rotate(x, cosine, sine):
         return x * cosine + pltpu.roll(x, HEAD_DIM // 2, 1) * sine
 
-    def halo(message, source, where, c):
-        part = pl.ds(c * half, half)
+    sent = []
+
+    def halo(message, source, where, c, used=None):
+        part = pl.ds(c * tile, tile)
         return pltpu.make_async_remote_copy(
             src_ref=kv.at[source, part], dst_ref=kv.at[message, part],
-            send_sem=ksend.at[message, c], recv_sem=krecv.at[message, c],
+            send_sem=ksend.at[message if used is None else used, c], recv_sem=krecv.at[message, c],
             device_id={"seq": where}, device_id_type=pl.DeviceIdType.MESH)
 
-    def send(condition, message, source, where, c):
+    def send(condition, message, source, where, c, used=None):
+        sent.append((condition, message, c, used))
+
         @pl.when(condition)
         def _():
-            halo(message, source, where, c).start()
+            halo(message, source, where, c, used).start()
 
     def got(message, c, condition=None):
         valid = z >= back[message]
+
         @pl.when(valid if condition is None else valid & condition)
         def _():
             halo(message, message, right, c).wait_recv()
 
-    for c in range(2):
-        for i in range(c * TILES // 2, (c + 1) * TILES // 2):
-            tok_copies[i].wait()
-            lax.fori_loop(i * (tile // 16), (i + 1) * (tile // 16), norm_rows, 0, unroll=2)
+    inner = (y == 1) | (y == 2)
+    outer = (y == 0) | (y == 3)
+    below = (z >= 1) & (z < z_last)
+
+    def from_z1(c):
+        got(Z1, c)
+        send(below, Z2, Z1, z_next, c)
+        send(z >= 1, R1, Z1, left, c)
+        send(z >= 1, L1, Z1, right, c)
+
+    def from_z2(c):
+        got(Z2, c)
+        send((z >= 2) & (y == 3), LA, Z2, right, c)
+
+    def from_la(c):
+        got(LA, c, inner)
+        send(inner, LX, LA, right, c)
+
+    def from_r1(c, condition):
+        got(R1, c, condition)
+        send(condition & (y < 3) & below, RA, R1, z_next, c, 9)
+        if c >= TILES // 2:
+            send(condition & (y == 1) & (z >= 1), LX, R1, left, c, 10)
+        send(condition & outer & (z >= 1), RX, R1, left, c)
+
+    def from_l1(c, condition):
+        got(L1, c, condition)
+        relays = outer if c < TILES // 2 else y == 0
+        send(condition & relays & (z >= 1), LX, L1, right, c)
+
+    def from_ra(c):
+        got(RA, c, y < 3)
+        send(inner & (z >= 2), RX, RA, left, c)
+
+    tables(0)
+    for c in range(TILES):
+        tok_copies[c].wait()
+        lax.fori_loop(c * (tile // 16), (c + 1) * (tile // 16), norm_rows, 0, unroll=2)
         if c == 0:
             wk_copy.wait()
             wv_copy.wait()
-        at = pl.ds(c * half, half)
+        else:
+            tables(c)
+        at = pl.ds(c * tile, tile)
         both = jnp.dot(nrm[at, :], wkv[...], preferred_element_type=F32)
         kv[0, at, :HEAD_DIM] = rotate(both[:, :HEAD_DIM], cos_s[at, :], sin_s[at, :]).astype(BF16)
         kv[0, at, HEAD_DIM:] = both[:, HEAD_DIM:].astype(BF16)
@@ -144,6 +188,7 @@
             q = rotate(both[:, j * 128:(j + 1) * 128], cos_s[...], sin_s[...]).astype(BF16)
             for t in range(TILES):
                 qs[t, h * tile:(h + 1) * tile, :] = q[t * tile:(t + 1) * tile, :]
+        from_z1(pair)
 
     factor = math.log2(math.e) / math.sqrt(HEAD_DIM)
     lanes = lax.broadcasted_iota(jnp.int32, (tile, HEAD_DIM), 1)
@@ -194,69 +239,51 @@
             unit(t, slot, first)
 
     order = [pick(y, options) for options in zip(
-        (Z1, R1, Z2, L1, RA, LA), (Z1, LA, R1, Z2, L1, RA),
+        (Z1, R1, L1, Z2, LA, RA), (Z1, LA, R1, Z2, L1, RA),
         (Z1, LA, R1, Z2, L1, RA), (Z1, LA, RA, R1, Z2, L1))]
-    inner = (y == 1) | (y == 2)
-    outer = (y == 0) | (y == 3)
-
-    def from_z1(c):
-        got(Z1, c)
-        send((z >= 1) & (z < z_last), Z2, Z1, z_next, c)
-        send(z >= 1, L1, Z1, right, c)
-        send(z >= 1, R1, Z1, left, c)
-
-    def from_z2(c):
-        got(Z2, c)
-        send((z >= 2) & (y > 0), RA, Z2, left, c)
-        send((z >= 2) & (y == 3), LA, Z2, right, c)
-
-    def from_la(c):
-        got(LA, c, inner)
-        send(inner, LX, LA, right, c)
-
-    def from_r1(c, condition):
-        got(R1, c, condition)
-        send(condition & outer & (z >= 1), RX, R1, left, c)
-
-    def from_l1(c):
-        got(L1, c)
-        send(outer & (z >= 1), LX, L1, right, c)
-
-    def from_ra(c, condition):
-        got(RA, c, condition)
-        send(condition & inner & (z >= 2), RX, RA, left, c)
-
-    from_z1(0)
+    always = y >= 0
+
+    def got_all(message, condition=None):
+        for c in range(TILES):
+            got(message, c, condition)
+
     sweep(0, True)
-    from_z1(1)
-    from_la(0)
-    from_la(1)
+    from_z1(2)
+    from_z1(3)
+    for c in range(TILES):
+        from_la(c)
     sweep(order[0])
+    from_r1(0, always)
+    from_r1(1, always)
     from_z2(0)
-    from_r1(0, y >= 0)
-    from_r1(1, y == 0)
-    got(LA, 0, y == 3)
-    got(LA, 1, y == 3)
+    from_r1(2, y == 0)
+    from_r1(3, y == 0)
+    got_all(LA, y == 3)
     sweep(order[1])
+    from_r1(2, y > 0)
     from_z2(1)
-    from_r1(1, y > 0)
-    from_l1(0)
-    from_ra(0, y == 3)
-    from_ra(1, y == 3)
+    from_l1(0, always)
+    from_l1(1, always)
+    from_r1(3, y > 0)
+    from_l1(2, y == 0)
+    from_l1(3, y == 0)
+    got_all(RA, y == 3)
     sweep(order[2])
-    from_l1(1)
+    from_z2(2)
+    from_l1(2, y > 0)
+    from_z2(3)
+    from_l1(3, y > 0)
     sweep(order[3])
-    from_ra(0, y < 3)
-    from_ra(1, y == 0)
+    from_ra(0)
+    got_all(LA, y == 0)
     sweep(order[4])
-    from_ra(1, inner)
-    got(LA, 0, y == 0)
-    got(LA, 1, y == 0)
+    from_ra(1)
+    from_ra(2)
+    from_ra(3)
     sweep(order[5])
-    last = (LX, RX)
-    for slot in last:
-        got(slot, 0)
-        got(slot, 1)
+    got_all(LX)
+    sweep(LX)
+    got_all(RX)
 
     half_tile = tile // 2
     upper, lower = pl.ds(0, half_tile), pl.ds(half_tile, half_tile)
@@ -307,47 +334,44 @@
             total = term if total is None else total + term
         return total
 
-    def project(t, early=None):
+    def begin(t):
+        for message in (2, 5, 6):
+            gather(t, message).wait_recv()
+        part[t] = partial(t, (0, 1, 2, 4, 5, 6))
+
+    def project(t):
         for message in (7, 8):
             gather(t, message).wait_recv()
-        total = partial(t, (3, 7)) + (partial_of(t) if early is None else early)
-        out_ref[t * tile:(t + 1) * tile, :] = total.astype(BF16)
-
-    def partial_of(t):
-        for message in (2, 5, 6):
-            gather(t, message).wait_recv()
-        return partial(t, (0, 1, 2, 4, 5, 6))
+        out_ref[t * tile:(t + 1) * tile, :] = (part[t] + partial(t, (3, 7))).astype(BF16)
 
     wo_copy.wait()
     for t in range(TILES):
-        for slot in last:
-            unit(t, slot, False)
+        unit(t, RX, False)
         finish(t)
-        if t >= 2:
-            relay(t - 2)
+    relay(0)
+    relay(1)
+    begin(0)
     relay(2)
+    begin(1)
+    relay(3)
+    begin(2)
     across(0)
+    begin(3)
+    across(1)
     project(0)
-    relay(3)
-    across(1)
+    across(2)
     project(1)
-    across(2)
+    across(3)
     project(2)
-    early = partial_of(3)
-    across(3)
-    project(3, early)
+    project(3)
 
     for t in range(TILES):
         for message in range(9):
             gather(t, message).wait_send()
-    sent = {Z1: z < z_last, Z2: (z >= 1) & (z < z_last), LA: (y < 3) | (z >= 2), L1: z >= 1,
-            LX: inner | (z >= 1), RA: (y == 0) | (z >= 2), R1: z >= 1,
-            RX: (outer & (z >= 1)) | (inner & (z >= 2))}
-    for message, condition in sent.items():
+    for condition, message, c, used in sent:
         @pl.when(condition)
         def _():
-            for c in range(2):
-                halo(message, message, right, c).wait_send()
+            halo(message, message, right, c, used).wait_send()
 
 
 def shards(tokens, norm_gain, query_weight, key_weight, value_weight, out_weight, segments):
@@ -360,7 +384,7 @@
     hbm = pl.BlockSpec(memory_space=pl.ANY)
     return pl.pallas_call(
         kernel,
-        out_shape=jax.ShapeDtypeStruct((rows, out_weight.shape[1]), BF16),
+        out_shape=pltpu.VMEM((rows, out_weight.shape[1]), BF16),
         in_specs=[hbm, vmem, vmem, vmem, hbm, hbm, hbm, hbm],
         out_specs=vmem,
         scratch_shapes=[
@@ -374,13 +398,14 @@
             pltpu.VMEM((TILES, heads * tile, HEAD_DIM), F32),
             pltpu.VMEM((TILES, heads * tile, 2 * HEAD_DIM), F32),
             pltpu.VMEM((TILES, 8, tile, heads * HEAD_DIM), BF16),
+            pltpu.VMEM((TILES, tile, out_weight.shape[1]), F32),
             pltpu.VMEM((rows, HEAD_DIM), F32),
             pltpu.VMEM((rows, HEAD_DIM), F32),
             pltpu.VMEM((rows, HEAD_DIM), jnp.int32),
             pltpu.SemaphoreType.DMA((TILES,)),
             pltpu.SemaphoreType.DMA((4,)),
-            pltpu.SemaphoreType.DMA((9, 2)),
-            pltpu.SemaphoreType.DMA((9, 2)),
+            pltpu.SemaphoreType.DMA((11, TILES)),
+            pltpu.SemaphoreType.DMA((9, TILES)),
             pltpu.SemaphoreType.DMA((TILES, 9)),
             pltpu.SemaphoreType.DMA((TILES, 9)),
         ],

time: 61.5 us -> 61 us (level)
  local copies, waits for them, and re-layouts: 1.87 us -> 0.8 us
    unnamed x1, local copies, waits for them, and re-layouts: 1.87 us -> 0.8 us
    pallas_call x1, Pallas kernels: 58.9 us -> 59.5 us  [shards(): pl.pallas_call(kernel, out_shape=pltpu.VMEM((rows, out_weight.shape[1]),...]
where the time goes in v3:
time: 61 us; the launch traced here: 60.9 us
  Pallas kernels  59.5 us (98%)
  local copies, waits for them, and re-layouts  0.8 us (1%)
    pallas_call x1, Pallas kernels, shards(): pl.pallas_call(kernel, out_shape=pltpu.VMEM((rows, out_weight.shape[1]),...  59.5 us

profile of v3, /device:TPU:65, one launch (start us, length us, event | category | flops | bytes accessed | tf_op | source)
XLA Modules:
  0.0 60.9 jit_solution(17962734174601941582)
XLA Ops:
  0.0 0.6 maximum_bitcast_fusion.freq_ref
  0.6 59.5 %shard_map.73 = bf16[512,512]{1,0:T(8,128)(2,1)S(1)} custom-call(bf16[512,4096]{1,0:T(8,128)(2,1)} %tok_hbm.1, f32[1,4096]{1,0:T(1,128)} %bitcast.5, f32[1,128]{1,0:T(1,128)} %maximum_bitcast_fusion.freq_ref, s32[128,128]{1,0:T(8,128)} %bitcast.4, bf16[4096,512]{1,0:T(8,128)(2,1)} %wq_hbm.1, bf16[4096,128]{1,0:T(8,128)(2,1)} %wk_hbm.1, ...), custom_call_target="tpu_custom_call" | custom-call | tf_op jit(solution)/shard_map/pallas_call | solution.py:385
  60.1 0.8 %copy.9 = bf16[512,512]{1,0:T(8,128)(2,1)} copy(bf16[512,512]{1,0:T(8,128)(2,1)S(1)} %shard_map.73) | data formatting | bytes 1048576
  (1 shorter events, 0.0 us)

commit v4 on v3

--- a/solution.py
+++ b/solution.py
@@ -139,6 +139,8 @@
 
     def from_z2(c):
         got(Z2, c)
+        if c < TILES // 2:
+            send((z >= 2) & (y >= 2), RA, Z2, left, c)
         send((z >= 2) & (y == 3), LA, Z2, right, c)
 
     def from_la(c):
@@ -147,7 +149,7 @@
 
     def from_r1(c, condition):
         got(R1, c, condition)
-        send(condition & (y < 3) & below, RA, R1, z_next, c, 9)
+        send(condition & ((y == 0) if c < TILES // 2 else (y < 3)) & below, RA, R1, z_next, c, 9)
         if c >= TILES // 2:
             send(condition & (y == 1) & (z >= 1), LX, R1, left, c, 10)
         send(condition & outer & (z >= 1), RX, R1, left, c)
@@ -157,28 +159,30 @@
         relays = outer if c < TILES // 2 else y == 0
         send(condition & relays & (z >= 1), LX, L1, right, c)
 
-    def from_ra(c):
-        got(RA, c, y < 3)
-        send(inner & (z >= 2), RX, RA, left, c)
+    def from_ra(c, condition):
+        got(RA, c, condition)
+        send(condition & (z >= 2), RX, RA, left, c)
 
     tables(0)
-    for c in range(TILES):
-        tok_copies[c].wait()
-        lax.fori_loop(c * (tile // 16), (c + 1) * (tile // 16), norm_rows, 0, unroll=2)
-        if c == 0:
-            wk_copy.wait()
-            wv_copy.wait()
-        else:
-            tables(c)
-        at = pl.ds(c * tile, tile)
+    for chunks in ((0,), (1,), (2, 3)):
+        for c in chunks:
+            tok_copies[c].wait()
+            lax.fori_loop(c * (tile // 16), (c + 1) * (tile // 16), norm_rows, 0, unroll=2)
+            if c == 0:
+                wk_copy.wait()
+                wv_copy.wait()
+            else:
+                tables(c)
+        at = pl.ds(chunks[0] * tile, len(chunks) * tile)
         both = jnp.dot(nrm[at, :], wkv[...], preferred_element_type=F32)
         kv[0, at, :HEAD_DIM] = rotate(both[:, :HEAD_DIM], cos_s[at, :], sin_s[at, :]).astype(BF16)
         kv[0, at, HEAD_DIM:] = both[:, HEAD_DIM:].astype(BF16)
-        if c == 0:
+        if chunks[0] == 0:
             pl.semaphore_wait(barrier, 7)
-        send(z < z_last, Z1, 0, z_next, c)
-        send(y < 3, LA, 0, right, c)
-        send(y == 0, RA, 0, left, c)
+        for c in chunks:
+            send(z < z_last, Z1, 0, z_next, c)
+            send(y < 3, LA, 0, right, c)
+            send(y == 0, RA, 0, left, c)
 
     wq_copy.wait()
     for pair in range(heads // 2):
@@ -188,7 +192,7 @@
             q = rotate(both[:, j * 128:(j + 1) * 128], cos_s[...], sin_s[...]).astype(BF16)
             for t in range(TILES):
                 qs[t, h * tile:(h + 1) * tile, :] = q[t * tile:(t + 1) * tile, :]
-        from_z1(pair)
+    from_z1(0)
 
     factor = math.log2(math.e) / math.sqrt(HEAD_DIM)
     lanes = lax.broadcasted_iota(jnp.int32, (tile, HEAD_DIM), 1)
@@ -239,8 +243,8 @@
             unit(t, slot, first)
 
     order = [pick(y, options) for options in zip(
-        (Z1, R1, L1, Z2, LA, RA), (Z1, LA, R1, Z2, L1, RA),
-        (Z1, LA, R1, Z2, L1, RA), (Z1, LA, RA, R1, Z2, L1))]
+        (Z1, R1, L1, Z2, LX, RA, LA), (Z1, LA, R1, Z2, L1, RA, LX),
+        (Z1, LA, R1, Z2, L1, RA, LX), (Z1, LA, RA, R1, Z2, L1, LX))]
     always = y >= 0
 
     def got_all(message, condition=None):
@@ -248,6 +252,7 @@
             got(message, c, condition)
 
     sweep(0, True)
+    from_z1(1)
     from_z1(2)
     from_z1(3)
     for c in range(TILES):
@@ -260,8 +265,8 @@
     from_r1(3, y == 0)
     got_all(LA, y == 3)
     sweep(order[1])
+    from_z2(1)
     from_r1(2, y > 0)
-    from_z2(1)
     from_l1(0, always)
     from_l1(1, always)
     from_r1(3, y > 0)
@@ -273,16 +278,18 @@
     from_l1(2, y > 0)
     from_z2(3)
     from_l1(3, y > 0)
+    from_ra(0, inner)
     sweep(order[3])
-    from_ra(0)
+    from_ra(1, inner)
+    from_ra(2, inner)
+    got_all(LX, y == 0)
+    sweep(order[4])
+    from_ra(3, inner)
+    got_all(RA, y == 0)
+    sweep(order[5])
+    got_all(LX, y > 0)
     got_all(LA, y == 0)
-    sweep(order[4])
-    from_ra(1)
-    from_ra(2)
-    from_ra(3)
-    sweep(order[5])
-    got_all(LX)
-    sweep(LX)
+    sweep(order[6])
     got_all(RX)
 
     half_tile = tile // 2

time: 61 us -> 58 us (0.951)
  Pallas kernels: 59.5 us -> 56.3 us
    pallas_call x1, Pallas kernels: 59.5 us -> 56.3 us  [shards(): pl.pallas_call(kernel, out_shape=pltpu.VMEM((rows, out_weight.shape[1]),...]
where the time goes in v4:
time: 58 us; the launch traced here: 57.7 us
  Pallas kernels  56.3 us (97%)
  local copies, waits for them, and re-layouts  0.8 us (1%)
  other arithmetic  0.6 us (1%)
    pallas_call x1, Pallas kernels, shards(): pl.pallas_call(kernel, out_shape=pltpu.VMEM((rows, out_weight.shape[1]),...  56.3 us

profile of v4, /device:TPU:65, one launch (start us, length us, event | category | flops | bytes accessed | tf_op | source)
XLA Modules:
  0.0 57.7 jit_solution(5278318986924181984)
XLA Ops:
  0.0 0.6 %maximum_bitcast_fusion.freq_ref = f32[1,128]{1,0:T(1,128)} fusion(f32[64]{0:T(128)S(1)} %negate_power_fusion), kind=kLoop, calls=%fused_computation | loop fusion | flops 128 | bytes 768 | tf_op jit(solution)/shard_map/broadcast_in_dim | solution.py:388
  0.6 56.3 %shard_map.73 = bf16[512,512]{1,0:T(8,128)(2,1)S(1)} custom-call(bf16[512,4096]{1,0:T(8,128)(2,1)} %tok_hbm.1, f32[1,4096]{1,0:T(1,128)} %bitcast.5, f32[1,128]{1,0:T(1,128)} %maximum_bitcast_fusion.freq_ref, s32[128,128]{1,0:T(8,128)} %bitcast.4, bf16[4096,512]{1,0:T(8,128)(2,1)} %wq_hbm.1, bf16[4096,128]{1,0:T(8,128)(2,1)} %wk_hbm.1, ...), custom_call_target="tpu_custom_call" | custom-call | tf_op jit(solution)/shard_map/pallas_call | solution.py:392
  56.9 0.8 %copy.9 = bf16[512,512]{1,0:T(8,128)(2,1)} copy(bf16[512,512]{1,0:T(8,128)(2,1)S(1)} %shard_map.73) | data formatting | bytes 1048576
  (1 shorter events, 0.0 us)

commit v5 on v4

--- a/solution.py
+++ b/solution.py
@@ -89,10 +89,10 @@
             pick(y, (1, 1, 0, 0)), pick(y, (2, 2, 1, 1))]
     side = [0, 0, 0, -1, -1, 1, 1, -2, 2]
     starts = [((z - back[s]) * 4 + lax.rem(y + side[s] + 4, 4)) * rows for s in range(9)]
-    for s in range(1, 9):
-        @pl.when(z < back[s])
-        def _():
-            kv[s] = jnp.zeros(kv.shape[1:], BF16)
+
+    @pl.when(z < back[RX])
+    def _():
+        kv[RX] = jnp.zeros(kv.shape[1:], BF16)
 
     def norm_rows(i, carry):
         at = pl.ds(pl.multiple_of(i * 16, 16), 16)
@@ -147,14 +147,16 @@
         got(LA, c, inner)
         send(inner, LX, LA, right, c)
 
-    def from_r1(c, condition):
-        got(R1, c, condition)
-        send(condition & ((y == 0) if c < TILES // 2 else (y < 3)) & below, RA, R1, z_next, c, 9)
+    def from_r1(c):
+        got(R1, c)
+        send(((y == 0) if c < TILES // 2 else (y < 3)) & below, RA, R1, z_next, c, 9)
         if c >= TILES // 2:
-            send(condition & (y == 1) & (z >= 1), LX, R1, left, c, 10)
-        send(condition & outer & (z >= 1), RX, R1, left, c)
-
-    def from_l1(c, condition):
+            send((y == 1) & (z >= 1), LX, R1, left, c, 10)
+
+    def pass_r1(c):
+        send(outer & (z >= 1), RX, R1, left, c)
+
+    def from_l1(c, condition=True):
         got(L1, c, condition)
         relays = outer if c < TILES // 2 else y == 0
         send(condition & relays & (z >= 1), LX, L1, right, c)
@@ -206,13 +208,15 @@
             value = jnp.where(slot == s, starts[s], value)
         return value
 
-    def unit(t, slot, first):
-        k = kv[slot, :, :HEAD_DIM]
-        v = jnp.concatenate([kv[slot, :, HEAD_DIM:], ones], axis=1)
-        low = low_s[t * tile:(t + 1) * tile, :] - start_of(slot)
+    def unit(t, slot, first, piece=None):
+        count = rows if piece is None else rows // 2
+        at = slice(None) if piece is None else pl.ds(piece * count, count)
+        k = kv[slot, at, :HEAD_DIM]
+        v = jnp.concatenate([kv[slot, at, HEAD_DIM:], ones[:count]], axis=1)
+        low = low_s[t * tile:(t + 1) * tile, :] - (start_of(slot) + (0 if piece is None else piece * count))
         s = lax.dot_general(qs[t], k, (((1,), (1,)), ((), ())), preferred_element_type=F32)
         chunks = []
-        for c in range(rows // 128):
+        for c in range(count // 128):
             ok = lanes + c * 128 >= low
             if first:
                 mine = lax.broadcasted_iota(jnp.int32, (tile, HEAD_DIM), 0) + t * tile
@@ -238,14 +242,15 @@
             acc[t, :, :HEAD_DIM] = acc[t, :, :HEAD_DIM] * decay + new[:, :HEAD_DIM]
             acc[t, :, HEAD_DIM:] = acc[t, :, HEAD_DIM:] * decay + new[:, HEAD_DIM:]
 
-    def sweep(slot, first=False):
-        for t in range(TILES):
-            unit(t, slot, first)
+    def sweep(slot, first=False, piece=None, condition=True):
+        @pl.when((start_of(slot) >= 0) & condition)
+        def _():
+            for t in range(TILES):
+                unit(t, slot, first, piece)
 
     order = [pick(y, options) for options in zip(
         (Z1, R1, L1, Z2, LX, RA, LA), (Z1, LA, R1, Z2, L1, RA, LX),
         (Z1, LA, R1, Z2, L1, RA, LX), (Z1, LA, RA, R1, Z2, L1, LX))]
-    always = y >= 0
 
     def got_all(message, condition=None):
         for c in range(TILES):
@@ -253,27 +258,32 @@
 
     sweep(0, True)
     from_z1(1)
+    sweep(Z1, piece=0)
     from_z1(2)
     from_z1(3)
     for c in range(TILES):
         from_la(c)
-    sweep(order[0])
-    from_r1(0, always)
-    from_r1(1, always)
+    sweep(Z1, piece=1)
     from_z2(0)
-    from_r1(2, y == 0)
-    from_r1(3, y == 0)
+    from_r1(0)
+    from_r1(1)
     got_all(LA, y == 3)
-    sweep(order[1])
+    sweep(order[1], condition=y > 0)
+    sweep(R1, piece=0, condition=y == 0)
     from_z2(1)
-    from_r1(2, y > 0)
-    from_l1(0, always)
-    from_l1(1, always)
-    from_r1(3, y > 0)
+    from_l1(0)
+    from_l1(1)
+    sweep(L1, piece=0, condition=y == 0)
+    from_r1(2)
+    from_r1(3)
+    for c in range(TILES):
+        pass_r1(c)
     from_l1(2, y == 0)
     from_l1(3, y == 0)
     got_all(RA, y == 3)
-    sweep(order[2])
+    sweep(order[2], condition=y > 0)
+    sweep(R1, piece=1, condition=y == 0)
+    sweep(L1, piece=1, condition=y == 0)
     from_z2(2)
     from_l1(2, y > 0)
     from_z2(3)

time: 58 us -> 58.1 us (level)
  no operation moved by 1% of the time
where the time goes in v5:
time: 58.1 us; the launch traced here: 58 us
  Pallas kernels  56.6 us (97%)
  local copies, waits for them, and re-layouts  0.8 us (1%)
  other arithmetic  0.6 us (1%)
    pallas_call x1, Pallas kernels, shards(): pl.pallas_call(kernel, out_shape=pltpu.VMEM((rows, out_weight.shape[1]),...  56.6 us

profile of v5, /device:TPU:65, one launch (start us, length us, event | category | flops | bytes accessed | tf_op | source)
XLA Modules:
  0.0 58.0 jit_solution(4451652238086020816)
XLA Ops:
  0.0 0.6 %maximum_bitcast_fusion.freq_ref = f32[1,128]{1,0:T(1,128)} fusion(f32[64]{0:T(128)S(1)} %negate_power_fusion), kind=kLoop, calls=%fused_computation | loop fusion | flops 128 | bytes 768 | tf_op jit(solution)/shard_map/broadcast_in_dim | solution.py:398
  0.6 56.6 %shard_map.73 = bf16[512,512]{1,0:T(8,128)(2,1)S(1)} custom-call(bf16[512,4096]{1,0:T(8,128)(2,1)} %tok_hbm.1, f32[1,4096]{1,0:T(1,128)} %bitcast.5, f32[1,128]{1,0:T(1,128)} %maximum_bitcast_fusion.freq_ref, s32[128,128]{1,0:T(8,128)} %bitcast.4, bf16[4096,512]{1,0:T(8,128)(2,1)} %wq_hbm.1, bf16[4096,128]{1,0:T(8,128)(2,1)} %wk_hbm.1, ...), custom_call_target="tpu_custom_call" | custom-call | tf_op jit(solution)/shard_map/pallas_call | solution.py:402
  57.2 0.8 %copy.9 = bf16[512,512]{1,0:T(8,128)(2,1)} copy(bf16[512,512]{1,0:T(8,128)(2,1)S(1)} %shard_map.73) | data formatting | bytes 1048576
  (1 shorter events, 0.0 us)

commit v6 on v5

--- a/solution.py
+++ b/solution.py
@@ -267,12 +267,12 @@
     from_z2(0)
     from_r1(0)
     from_r1(1)
+    from_l1(0)
     got_all(LA, y == 3)
     sweep(order[1], condition=y > 0)
     sweep(R1, piece=0, condition=y == 0)
+    from_l1(1)
     from_z2(1)
-    from_l1(0)
-    from_l1(1)
     sweep(L1, piece=0, condition=y == 0)
     from_r1(2)
     from_r1(3)
@@ -282,8 +282,13 @@
     from_l1(3, y == 0)
     got_all(RA, y == 3)
     sweep(order[2], condition=y > 0)
-    sweep(R1, piece=1, condition=y == 0)
-    sweep(L1, piece=1, condition=y == 0)
+
+    @pl.when((start_of(R1) >= 0) & (y == 0))
+    def _():
+        for t in range(TILES):
+            unit(t, R1, False, 1)
+            unit(t, L1, False, 1)
+
     from_z2(2)
     from_l1(2, y > 0)
     from_z2(3)

time: 58.1 us -> 57.3 us (0.986)
  Pallas kernels: 56.6 us -> 55.7 us
    pallas_call x1, Pallas kernels: 56.6 us -> 55.7 us  [shards(): pl.pallas_call(kernel, out_shape=pltpu.VMEM((rows, out_weight.shape[1]),...]
where the time goes in v6:
time: 57.3 us; the launch traced here: 57.1 us
  Pallas kernels  55.7 us (97%)
  local copies, waits for them, and re-layouts  0.8 us (1%)
  other arithmetic  0.6 us (1%)
    pallas_call x1, Pallas kernels, shards(): pl.pallas_call(kernel, out_shape=pltpu.VMEM((rows, out_weight.shape[1]),...  55.7 us

profile of v6, /device:TPU:65, one launch (start us, length us, event | category | flops | bytes accessed | tf_op | source)
XLA Modules:
  0.0 57.1 jit_solution(11063219499783530949)
XLA Ops:
  0.0 0.6 %maximum_bitcast_fusion.freq_ref = f32[1,128]{1,0:T(1,128)} fusion(f32[64]{0:T(128)S(1)} %negate_power_fusion), kind=kLoop, calls=%fused_computation | loop fusion | flops 128 | bytes 768 | tf_op jit(solution)/shard_map/broadcast_in_dim | solution.py:403
  0.6 55.7 %shard_map.73 = bf16[512,512]{1,0:T(8,128)(2,1)S(1)} custom-call(bf16[512,4096]{1,0:T(8,128)(2,1)} %tok_hbm.1, f32[1,4096]{1,0:T(1,128)} %bitcast.5, f32[1,128]{1,0:T(1,128)} %maximum_bitcast_fusion.freq_ref, s32[128,128]{1,0:T(8,128)} %bitcast.4, bf16[4096,512]{1,0:T(8,128)(2,1)} %wq_hbm.1, bf16[4096,128]{1,0:T(8,128)(2,1)} %wk_hbm.1, ...), custom_call_target="tpu_custom_call" | custom-call | tf_op jit(solution)/shard_map/pallas_call | solution.py:407
  56.3 0.8 %copy.9 = bf16[512,512]{1,0:T(8,128)(2,1)} copy(bf16[512,512]{1,0:T(8,128)(2,1)S(1)} %shard_map.73) | data formatting | bytes 1048576
  (1 shorter events, 0.0 us)
